TPU v7x, 32 devices: a whole 2x2x4 slice. The times are simulated.
32 devices in a mesh: dp: 16 (over z, y, x), mp: 2 (over core).
Axes of the slice: x: 2, y: 2, z: 4, core: 2. Of those that a mesh axis runs over, the one named last changes fastest.
Arguments:
- hidden: bfloat16 [2, 64, 64, 768], P(None, 'dp'), may hold values from -6 to 6
- encoder_tokens: bfloat16 [2, 32, 576, 768], P(None, 'dp'), may hold values from -6 to 6
- segment_ids: int32 [2, 64, 64], P(None, 'dp'), may hold values from 0 to 3, never falling along the last dimension, each value on 1 to 32 neighbouring positions
- image_index: int32 [2, 64], P(None, 'dp'), may hold values from 0 to 1
- cotangent: bfloat16 [2, 64, 64, 768], P(None, 'dp'), may hold values from -6 to 6
- norm_gains: bfloat16 [3, 768], P(None, 'dp'), may hold values from 0.099609375 to 1.8984375
- qkv_weight: bfloat16 [3, 768, 768], P(None, 'dp', 'mp'), may hold values from -0.21875 to 0.21875
- self_out_weight: bfloat16 [768, 768], P('dp', 'mp'), may hold values from -0.875 to 0.875
- cross_query_weight: bfloat16 [768, 768], P('dp', 'mp'), may hold values from -0.21875 to 0.21875
- cross_kv_weight: bfloat16 [2, 768, 768], P(None, 'dp', 'mp'), may hold values from -0.21875 to 0.21875
- cross_out_weight: bfloat16 [768, 768], P('dp', 'mp'), may hold values from -2.5 to 2.5
- up_weight: bfloat16 [768, 3072], P('dp', 'mp'), may hold values from -0.21875 to 0.21875
- down_weight: bfloat16 [768, 3072], P('dp', 'mp'), may hold values from -0.109375 to 0.109375
Outputs:
- output: bfloat16 [2, 64, 64, 768], P(None, 'dp')
- input_grad: float32 [2, 64, 64, 768], P(None, 'dp')
- encoder_grad: float32 [2, 32, 576, 768], P(None, 'dp', None, 'mp')
- grad_norm_gains: float32 [3, 768], P(None, 'dp')
- grad_qkv: float32 [3, 768, 768], P(None, 'dp', 'mp')
- grad_self_out: float32 [768, 768], P('dp', 'mp')
- grad_cross_query: float32 [768, 768], P('dp', 'mp')
- grad_cross_kv: float32 [2, 768, 768], P(None, 'dp', 'mp')
- grad_cross_out: float32 [768, 768], P('dp', 'mp')
- grad_up: float32 [768, 3072], P('dp', 'mp')
- grad_down: float32 [768, 3072], P('dp', 'mp')
Inputs may be any that keep to these rules, and one draw needn't show every extreme that they name: `segment_ids`: within a row the ids never fall; they number the 4 captions of the row, each of 1 to 32 tokens. Caption row r of a micro-batch reads image (r // 4) * 2 + image_index of that row.
All inputs are finite; a program needn't handle non-finite values.
Results may differ from a plain program's by a relative error of at most 0.019.
Values may be sent and summed in bfloat16 or wider, within the bound.
A program may use at most 192 MiB of HBM per device.

v0:
```python
import functools
from types import SimpleNamespace

import jax
import jax.numpy as jnp
from jax import lax
from jax.experimental import pallas as pl
from jax.experimental.pallas import tpu as pltpu
from jax.sharding import PartitionSpec as P

HEAD = 64
PAIR = 2 * HEAD
EPSILON = 1e-05
NEGATIVE = -1e30
ROOT_HALF = 0.7071067811865476
DENSITY = 0.3989422804014327
MESH = pl.DeviceIdType.MESH
LOW = jnp.bfloat16
F32 = jnp.float32
QKV, SO, CQ, CKV, CO, MATS = 0, 3, 4, 5, 7, 8
DIRECT = ("q", "k", "v")
UP, DOWN = 0, 1
LN_ROWS = 128
TILE = 256


def dot(left, right, left_dim, right_dim):
    return lax.dot_general(
        left, right, (((left_dim,), (right_dim,)), ((), ())), preferred_element_type=F32
    )


def lanes_of(pair):
    return pl.ds(pair * PAIR, PAIR)


def head_masks():
    lane = lax.broadcasted_iota(jnp.int32, (1, PAIR), 1)
    first = jnp.where(lane < HEAD, 1.0, 0.0)
    return first.astype(LOW), (1.0 - first).astype(LOW)


def stack_heads(values, masks):
    return jnp.concatenate([values * masks[0], values * masks[1]], axis=0)


def join_heads(stacked):
    half = stacked.shape[0] // 2
    lane = lax.broadcasted_iota(jnp.int32, (half, PAIR), 1)
    return jnp.where(lane < HEAD, stacked[:half], stacked[half:])


def centre(values):
    centred = values - jnp.mean(values, axis=-1, keepdims=True)
    spread = jnp.mean(centred * centred, axis=-1, keepdims=True)
    scale = lax.rsqrt(spread + EPSILON)
    return centred * scale, scale


def softmax_keys(scores):
    shifted = jnp.exp(scores - jnp.max(scores, axis=0, keepdims=True))
    return shifted / jnp.sum(shifted, axis=0, keepdims=True)


def layer(g, *refs):
    r = SimpleNamespace(**dict(zip(g.names, refs)))
    me, mp = lax.axis_index("dp"), lax.axis_index("mp")
    zi, col = me // 4, me % 4
    sibling = (me, 1 - mp)
    col_x = col + 1 - 2 * (col % 2)
    col_y = (col + 2) % 4
    col_d = (col_x + 2) % 4
    col_a = mp * col_x + (1 - mp) * col_y
    col_b = mp * col_y + (1 - mp) * col_x
    at_x, at_y = (zi * 4 + col_x, mp), (zi * 4 + col_y, mp)
    at_a, at_b = (zi * 4 + col_a, mp), (zi * 4 + col_b, mp)
    z_of = [(zi + k) % g.nz for k in range(1, g.nz)]
    z_from = [(zi + g.nz - k) % g.nz for k in range(1, g.nz)]
    at_z = [(z * 4 + col, mp) for z in z_of]

    greeted = [sibling] + ([at_x, at_y] + at_z if g.comm else [])
    barrier = pltpu.get_barrier_semaphore()
    for device in greeted:
        pl.semaphore_signal(barrier, inc=1, device_id=device, device_id_type=MESH)

    def remote(src, dst, send, recv, device):
        return pltpu.make_async_remote_copy(
            src_ref=src, dst_ref=dst, send_sem=send, recv_sem=recv, device_id=device, device_id_type=MESH
        )

    local = []

    def bring(src, dst):
        copy = pltpu.make_async_copy(src, dst, r.local_sem.at[len(local)])
        copy.start()
        local.append(copy)
        return copy

    def slot(first, count):
        ref = r.w8.at[pl.ds(first, count)]
        return ref.at[:, zi, col] if g.comm else ref

    def wide_slot(which):
        return r.wf.at[which, zi, col] if g.comm else r.wf.at[which]

    weights = [
        bring(r.qkv_in, slot(QKV, 3)),
        bring(r.so_in, slot(SO, 1)),
        bring(r.cq_in, slot(CQ, 1)),
        bring(r.ckv_in, slot(CKV, 2)),
        bring(r.co_in, slot(CO, 1)),
        bring(r.up_in, wide_slot(UP)),
        bring(r.down_in, wide_slot(DOWN)),
    ]
    bring_hidden = bring(r.hidden_in, r.hidden)
    bring_enc = bring(r.enc_in, r.enc)
    bring_cot = bring(r.cot_in, r.cot)

    half = g.ff // 2

    def mats(first, ref, at):
        part = pl.ds(first, 1)

        def each(c, body):
            @pl.loop(0, g.nz)
            def _(z):
                body(r.p8.at[first, z, c], lambda landed: landed.at[0, z])

        return SimpleNamespace(
            src=lambda: ref.at[pl.ds(at, 1)],
            w=lambda z, c: r.w8.at[part, z, c], w_column=lambda c: r.w8.at[part, :, c],
            w_row=lambda z: r.w8.at[part, z], p_row=lambda z: r.p8.at[part, z],
            p=lambda z, c: r.p8.at[part, z, c], p_column=lambda c: r.p8.at[part, :, c],
            lb=lambda k: r.lb8.at[k, part], la=lambda: r.la8.at[part], lz=lambda k: r.lz8.at[k, part],
            lx=lambda: r.lx8.at[part], in_row=lambda row, c: row.at[:, c],
            tz=lambda k: r.turn8_z.at[k], tb=lambda k: r.turn8_b.at[k], ta=lambda: r.turn8_a,
            tx=lambda: r.turn8_x, each=each, sum=lambda: r.g8.at[part], sum_out=lambda: r.g8_out.at[part],
        )

    def strip(which, first, i, ref):
        cols = pl.ds(first, half)

        def each(c, body):
            @pl.loop(0, g.nz)
            def _(z):
                body(r.pf.at[which, z, c, :, cols], lambda landed: landed.at[z])

        return SimpleNamespace(
            src=lambda: ref.at[:, cols],
            w=lambda z, c: r.wf.at[which, z, c, :, cols], w_column=lambda c: r.wf.at[which, :, c, :, cols],
            w_row=lambda z: r.wf.at[which, z, :, :, cols], p_row=lambda z: r.pf.at[which, z, :, :, cols],
            p=lambda z, c: r.pf.at[which, z, c, :, cols], p_column=lambda c: r.pf.at[which, :, c, :, cols],
            lb=lambda k: r.lbf.at[k, i], la=lambda: r.laf.at[i], lz=lambda k: r.lzf.at[k, i],
            lx=lambda: r.lxf.at[i], in_row=lambda row, c: row.at[c],
            tz=lambda k: r.turnf_z.at[k], tb=lambda k: r.turnf_b.at[k], ta=lambda: r.turnf_a,
            tx=lambda: r.turnf_x, each=each, sum=lambda: r.gf.at[which, :, cols],
            sum_out=lambda: r.gf_out.at[which, :, cols],
        )

    groups = dict(
        q=mats(QKV, r.qkv_in, 0), k=mats(QKV + 1, r.qkv_in, 1), v=mats(QKV + 2, r.qkv_in, 2),
        ck=mats(CKV, r.ckv_in, 0), cv=mats(CKV + 1, r.ckv_in, 1),
        so=mats(SO, r.so_in, 0), cq=mats(CQ, r.cq_in, 0), co=mats(CO, r.co_in, 0),
        up0=strip(UP, 0, 0, r.up_in), up1=strip(UP, half, 1, r.up_in),
        dn0=strip(DOWN, 0, 2, r.down_in), dn1=strip(DOWN, half, 3, r.down_in),
    )
    for i, (name, group) in enumerate(groups.items()):
        group.i, group.turned, group.direct = i, name in ("co", "dn1"), name in DIRECT

    inner = (zi == 1) | (zi == 2)
    goes = (zi != 3, None, zi != 0)
    hops = range(3)
    other = 3 * (2 - zi)
    onward = 3 * (zi - 1)
    filled = 2 * jnp.where(zi == 0, 1, 0)

    written = []

    def write(src, dst):
        copy = pltpu.make_async_copy(src, dst, r.write_sem.at[len(written)])
        copy.start()
        written.append(copy)

    started = []

    def only(condition, act):
        if condition is None:
            act()
        else:
            pl.when(condition)(act)

    def start(copy, condition=None):
        only(condition, copy.start)
        started.append((copy, condition))

    def arrived(ref, send, recv, device, condition=None):
        only(condition, remote(ref, ref, send, recv, device).wait_recv)

    def gather_z(name):
        t = groups[name]
        for k in hops:
            src, dst = (t.w_row(zi), t.w_row(zi)) if t.turned else (t.src(), t.w(zi, col))
            start(remote(src, dst, r.agz_s.at[t.i, k], r.agz_r.at[t.i, k], at_z[k]), None if t.direct else goes[k])

    def z_part(t, z):
        return t.w_row(z) if t.turned else t.w(z, col)

    def gather_on(name):
        t = groups[name]
        arrived(z_part(t, z_from[1]), r.agz_s.at[t.i, 1], r.agz_r.at[t.i, 1], at_z[1])
        if t.direct:
            return
        part = z_part(t, jnp.where(inner, other, 0))
        start(
            remote(part, part, r.agz_s.at[t.i, 3], r.agz_r.at[t.i, 2 * jnp.where(zi == 2, 1, 0)],
                   (jnp.where(inner, onward, 0) * 4 + col, mp)),
            inner,
        )

    def to_both(t, i, src, dst):
        start(remote(src, dst, r.aga_s.at[t.i, i], r.aga_r.at[t.i, i], at_a))
        start(remote(src, dst, r.agb_s.at[t.i, i], r.agb_r.at[t.i, i], at_b))

    def gather_own(name):
        t = groups[name]
        to_both(t, 0, t.src(), t.w(zi, col))

    def gather_a(name):
        t = groups[name]
        for k in (1, 0, 2):
            block = t.w(z_from[k], col)
            if k != 1:
                arrived(block, r.agz_s.at[t.i, k], r.agz_r.at[t.i, k], at_z[k])
            to_both(t, 1 + k, block, block)

    def gather_b(name):
        t = groups[name]
        arrived(t.w(zi, col_a), r.aga_s.at[t.i, 0], r.aga_r.at[t.i, 0], at_a)
        part = t.w(zi, col_a)
        if not t.turned:
            for k in hops:
                arrived(t.w(z_from[k], col_a), r.aga_s.at[t.i, 1 + k], r.aga_r.at[t.i, 1 + k], at_a)
            part = t.w_column(col_a)
        start(remote(part, part, r.agb_s.at[t.i, 4], r.agb_r.at[t.i, 4], at_b))

    def gather_end(name):
        t = groups[name]
        arrived(t.w(zi, col_b), r.agb_s.at[t.i, 0], r.agb_r.at[t.i, 0], at_b)
        if not t.turned:
            for k in hops:
                arrived(t.w(z_from[k], col_b), r.agb_s.at[t.i, 1 + k], r.agb_r.at[t.i, 1 + k], at_b)
        part = t.w(zi, col_d) if t.turned else t.w_column(col_d)
        arrived(part, r.agb_s.at[t.i, 4], r.agb_r.at[t.i, 4], at_b)

    def gather_turn(name):
        gather_end(name)
        gather_z(name)

    def gather_turned(name):
        t = groups[name]
        for k in (0, 2):
            arrived(t.w_row(z_from[k]), r.agz_s.at[t.i, k], r.agz_r.at[t.i, k], at_z[k])

    def added(target, *landed):
        total = target[...].astype(F32)
        for ref in landed:
            total = total + ref[...].astype(F32)
        return total

    def z_start(t, part, place):
        for k in hops:
            condition = None if t.direct else jnp.logical_not(inner) if k == 1 else goes[k]
            start(remote(part(z_of[k]), place(k), r.rsz_s.at[t.i, k], r.rsz_r.at[t.i, k], at_z[k]), condition)
        if t.direct:
            return
        end_part = part(jnp.where(inner, 0, 3 - zi))
        beside = (jnp.where(zi == 0, 1, 2) * 4 + col, mp)
        extra = t.tx() if t.turned else t.lx()
        start(remote(end_part, extra, r.rsz_s.at[t.i, 3], r.rsz_r.at[t.i, 3], beside), jnp.logical_not(inner))

    def reduce_b(name):
        t = groups[name]
        if t.turned:
            z_start(t, t.p_row, t.tz)
            return
        for k, c in enumerate((col_b, col_d)):
            start(remote(t.p_column(c), t.lb(k), r.rsb_s.at[t.i, k], r.rsb_r.at[t.i, k], at_b))

    def reduce_on(name):
        t = groups[name]
        if t.direct:
            return
        far = z_of[1]
        extra = t.tx() if t.turned else t.lx()

        @pl.when(inner)
        def _():
            arrived(extra, r.rsz_s.at[t.i, 3], r.rsz_r.at[t.i, 3], at_z[1])
            if t.turned:
                @pl.loop(0, 4)
                def _(c):
                    target = t.p(far, c)
                    target[...] = added(target, t.in_row(extra, c)).astype(LOW)
            else:
                target = t.p(far, col)
                target[...] = added(target, extra).astype(LOW)

        part, place = (t.p_row(far), t.tz(1)) if t.turned else (t.p(far, col), t.lz(1))
        start(remote(part, place, r.rsz_s.at[t.i, 1], r.rsz_r.at[t.i, 1], at_z[1]), inner)

    def z_arrived(t, place):
        places = ((0, None), (1, None), (2, None)) if t.direct else ((1, None), (filled, None), (2, inner))
        for k, condition in places:
            arrived(place(k), r.rsz_s.at[t.i, k], r.rsz_r.at[t.i, k], at_z[1], condition)

    def reduce_turn(name):
        t = groups[name]
        z_arrived(t, t.tz)

        @pl.loop(0, 4)
        def _(c):
            target = t.p(zi, c)
            target[...] = added(target, t.in_row(t.tz(1), c), t.in_row(t.tz(filled), c)).astype(LOW)

        @pl.when(inner)
        def _():
            @pl.loop(0, 4)
            def _(c):
                target = t.p(zi, c)
                target[...] = added(target, t.in_row(t.tz(2), c)).astype(LOW)

        for k, c in enumerate((col_b, col_d)):
            start(remote(t.p(zi, c), t.tb(k), r.rsb_s.at[t.i, k], r.rsb_r.at[t.i, k], at_b))

    def reduce_a(name):
        t = groups[name]
        for k, c in ((1, col_a), (0, col)):
            landed = t.tb(k) if t.turned else t.lb(k)
            arrived(landed, r.rsb_s.at[t.i, k], r.rsb_r.at[t.i, k], at_b)
            if t.turned:
                target = t.p(zi, c)
                target[...] = added(target, landed).astype(LOW)
            else:
                def add(target, view):
                    target[...] = added(target, view(landed)).astype(LOW)
                t.each(c, add)
            if k:
                src, dst = (t.p(zi, c), t.ta()) if t.turned else (t.p_column(c), t.la())
                start(remote(src, dst, r.rsa_s.at[t.i], r.rsa_r.at[t.i], at_a))

    def reduce_z(name):
        t = groups[name]
        landed = t.la()
        arrived(landed, r.rsa_s.at[t.i], r.rsa_r.at[t.i], at_a)

        def add(target, view):
            target[...] = added(target, view(landed)).astype(LOW)
        t.each(col, add)
        z_start(t, lambda z: t.p(z, col), t.lz)

    def reduce_end(name):
        t = groups[name]
        total = t.sum()
        if t.turned:
            arrived(t.ta(), r.rsa_s.at[t.i], r.rsa_r.at[t.i], at_a)
            total[...] = added(t.p(zi, col), t.ta())
        else:
            z_arrived(t, t.lz)
            if t.direct:
                total[...] = added(t.p(zi, col), t.lz(0), t.lz(1), t.lz(2))
            else:
                total[...] = added(t.p(zi, col), t.lz(1), t.lz(filled))

                @pl.when(inner)
                def _():
                    total[...] = added(total, t.lz(2))
        write(total, t.sum_out())

    def move(*steps):
        if g.comm:
            for step, name in zip(steps[::2], steps[1::2]):
                step(name)

    def w8(j):
        return r.w8[j].reshape(g.d, g.f)

    def wide(which, cols):
        if g.comm:
            return r.wf[which, :, :, :, cols].reshape(g.d, -1)
        return r.wf[which, :, cols]

    def put8(j, value):
        r.p8[j] = value.astype(LOW).reshape(r.p8.shape[1:])

    def put_wide(which, cols, value):
        if g.comm:
            r.pf[which, :, :, :, cols] = value.astype(LOW).reshape(g.nz, 4, g.blk, -1)
        else:
            r.pf[which, :, cols] = value.astype(LOW)

    part = g.t // 2

    def exchange(e, i):
        rows = pl.ds(i * part, part)
        return remote(
            r.stage.at[e % 2, rows], r.land.at[e % 3, rows], r.ex_s.at[e, i], r.ex_r.at[e, i], sibling
        )

    def exchange_start(e, product):
        for i in range(2):
            rows = pl.ds(i * part, part)
            r.stage[e % 2, rows] = product(rows).astype(LOW)
            exchange(e, i).start()

    def by_rows(e, body):
        for i in range(2):
            exchange(e, i).wait_recv()
            exchange(e, i).wait_send()

            @pl.loop(0, part // LN_ROWS)
            def _(n):
                rows = pl.ds(pl.multiple_of(i * part + n * LN_ROWS, LN_ROWS), LN_ROWS)
                body(rows, r.stage[e % 2, rows].astype(F32) + r.land[e % 3, rows].astype(F32))

    def norm(values, i):
        return (centre(values)[0] * r.gains[i]).astype(LOW)

    def norm_back(i, values, grad):
        normed, scale = centre(values)
        r.gain_sum[i] += jnp.sum((grad * normed).reshape(-1, 8, g.d), axis=0)
        scaled = grad * r.gains[i]
        return scale * (
            scaled
            - jnp.mean(scaled, axis=-1, keepdims=True)
            - normed * jnp.mean(scaled * normed, axis=-1, keepdims=True)
        )

    masks = head_masks()
    score_scale = HEAD ** (-0.5)
    pairs = g.f // PAIR

    pl.semaphore_wait(barrier, len(greeted))
    small = []

    def meet(src, dst, device):
        i = len(small)
        copy = remote(src, dst, r.small_s.at[i], r.small_r.at[i], device)
        copy.start()
        small.append(copy)
        return copy

    if g.comm:
        spot = lax.broadcasted_iota(jnp.int32, (g.blk, g.d), 0) + me * g.blk
        place = jnp.where(spot == lax.broadcasted_iota(jnp.int32, (g.blk, g.d), 1), 1.0, 0.0).astype(LOW)
        r.gain_pass[0, 0:3] = dot(r.gains_in[...], place, 1, 0).astype(LOW)
        for k in hops:
            meet(r.gain_pass.at[0], r.gain_land.at[k], at_z[k])
    move(
        gather_z, "q", gather_own, "q", gather_own, "co", gather_own, "dn1", gather_z, "k", gather_own, "k",
        gather_own, "v", gather_own, "ck", gather_own, "cv", gather_own, "so", gather_own, "cq",
    )
    for copy in weights:
        copy.wait()
    total = r.gain_pass[0, 0:3].astype(F32) if g.comm else r.gains_in[...].astype(F32)
    if g.comm:
        for k in hops:
            small[k].wait_recv()
            total = total + r.gain_land[k, 0:3].astype(F32)
        r.gain_pass[1, 0:3] = total.astype(LOW)
        hop = meet(r.gain_pass.at[1], r.gain_land.at[3], at_x)
    r.bias[...] = jnp.full(r.bias.shape, NEGATIVE)
    key = lax.broadcasted_iota(jnp.int32, (g.seq, g.seq), 0)
    query = lax.broadcasted_iota(jnp.int32, (g.seq, g.seq), 1)
    for row in range(g.rows):
        across = r.seg[row // g.row_mb, row % g.row_mb:row % g.row_mb + 1, :].astype(F32)
        down = jnp.sum(jnp.where(key == query, across, 0.0), axis=1, keepdims=True)
        p, at = row * g.seq // PAIR, row * g.seq % PAIR
        r.bias[p, at:at + g.seq, at:at + g.seq] = jnp.where((key <= query) & (down == across), 0.0, NEGATIVE)
    r.gain_sum[...] = jnp.zeros_like(r.gain_sum)
    move(gather_b, "co", gather_on, "q", gather_a, "q", gather_b, "dn1", gather_z, "v")
    if g.comm:
        hop.wait_recv()
        total = total + r.gain_land[3, 0:3].astype(F32)
        r.gain_pass[2, 0:3] = total.astype(LOW)
        hop = meet(r.gain_pass.at[2], r.gain_land.at[4], at_y)
    move(gather_on, "k", gather_a, "k", gather_z, "ck")
    if g.comm:
        hop.wait_recv()
        total = total + r.gain_land[4, 0:3].astype(F32)
    for i in range(3):
        r.gains[i] = total[i:i + 1]
    bring_hidden.wait()

    @pl.loop(0, g.t // LN_ROWS)
    def _(n):
        rows = pl.ds(pl.multiple_of(n * LN_ROWS, LN_ROWS), LN_ROWS)
        r.a1[rows] = norm(r.hidden[rows].astype(F32), 0)

    def project(j):
        r.qkv[j] = dot(r.a1[...], w8(QKV + j), 1, 0).astype(LOW)

    move(
        gather_on, "v", gather_a, "v", gather_z, "cv", gather_b, "q", gather_on, "ck", gather_z, "so",
        gather_b, "k", gather_on, "cv", gather_z, "cq", gather_a, "ck", gather_b, "v", gather_on, "so",
        gather_z, "up0", gather_a, "cv", gather_end, "q",
    )
    project(0)
    move(
        gather_on, "cq", gather_turn, "co", gather_z, "up1", gather_b, "ck", gather_a, "so",
        gather_own, "up0", gather_end, "k",
    )
    project(1)
    move(
        gather_b, "cv", gather_on, "up0", gather_z, "dn0", gather_a, "cq", gather_own, "up1", gather_b, "so",
        gather_end, "v",
    )
    project(2)

    def self_attend(first, last):
        @pl.loop(first, last)
        def _(p):
            rows = pl.ds(pl.multiple_of(p * PAIR, PAIR), PAIR)
            bias = jnp.concatenate([r.bias[p]] * 2, axis=1)
            for h in range(pairs):
                lanes = lanes_of(h)
                queries = stack_heads(r.qkv[0, rows, lanes], masks)
                scores = dot(r.qkv[1, rows, lanes], queries, 1, 1) * score_scale + bias
                weights_low = softmax_keys(scores).astype(LOW)
                r.self_p[p, h] = weights_low
                r.mixed[rows, lanes] = join_heads(dot(weights_low, r.qkv[2, rows, lanes], 0, 0)).astype(LOW)

    def project_images(m):
        @pl.loop(0, g.images)
        def _(image):
            rows = pl.ds(pl.multiple_of(image * g.ctx, g.ctx), g.ctx)
            r.kv[m, image] = dot(r.enc[rows], w8(CKV + m), 1, 0).astype(LOW)

    self_attend(0, g.t // PAIR)
    bring_enc.wait()
    move(gather_b, "cq", gather_on, "co", gather_end, "ck")
    project_images(0)
    move(gather_a, "up0", gather_on, "up1", gather_own, "dn0", gather_end, "cv")
    project_images(1)
    move(gather_on, "dn0", gather_turn, "dn1", gather_end, "so")
    exchange_start(0, lambda rows: dot(r.mixed[rows], w8(SO), 1, 1))

    def after_self(rows, total):
        resid = r.hidden[rows].astype(F32) + total
        r.resid_one[rows] = resid
        r.a2[rows] = norm(resid, 1)

    move(gather_a, "up1")
    by_rows(0, after_self)
    move(gather_b, "up0", gather_a, "dn0", gather_end, "cq")
    r.cq[...] = dot(r.a2[...], w8(CQ), 1, 0).astype(LOW)

    def cross_attend(first, last):
        @pl.loop(first, last)
        def _(row):
            rows = pl.ds(pl.multiple_of(row * g.seq, g.seq), g.seq)
            image = (row // g.row_mb) * g.img_mb + r.image_ids[row // g.row_mb, row % g.row_mb]
            for h in range(pairs):
                lanes = lanes_of(h)
                queries = stack_heads(r.cq[rows, lanes], masks)
                scores = dot(r.kv[0, image, :, lanes], queries, 1, 1) * score_scale
                weights_low = softmax_keys(scores).astype(LOW)
                r.cross_p[row * pairs + h] = weights_low
                r.cmixed[rows, lanes] = join_heads(dot(weights_low, r.kv[1, image, :, lanes], 0, 0)).astype(LOW)

    cross_attend(g.rows * 0 // 2, g.rows * 1 // 2)
    cross_attend(g.rows * 1 // 2, g.rows * 2 // 2)
    move(gather_b, "up1", gather_turned, "co")
    exchange_start(1, lambda rows: dot(r.cmixed[rows], w8(CO), 1, 1))

    def after_cross(rows, total):
        resid = r.resid_one[rows] + total
        r.resid_two[rows] = resid
        r.a3[rows] = norm(resid, 2)

    move(gather_b, "dn0", gather_on, "dn1")
    by_rows(1, after_cross)
    bring_cot.wait()

    def up_half(first):
        @pl.loop(0, half // TILE)
        def _(n):
            cols = pl.ds(pl.multiple_of(first + n * TILE, TILE), TILE)
            pre = dot(r.a3[...], wide(UP, cols), 1, 0)
            below = 0.5 * (1.0 + lax.erf(pre * ROOT_HALF))
            r.act[:, cols] = (pre * below).astype(LOW)
            slope = below + pre * (DENSITY * jnp.exp(-0.5 * (pre * pre)))
            r.slope[:, cols] = slope.astype(r.slope.dtype)

    def grad_wide(which, left, right, first):
        cols = pl.ds(first, half)
        put_wide(which, cols, dot(left[...], right[:, cols], 0, 0))

    def down_half(first):
        @pl.loop(0, half // TILE)
        def _(n):
            cols = pl.ds(pl.multiple_of(first + n * TILE, TILE), TILE)
            grad_act = dot(r.cot[...], wide(DOWN, cols), 1, 0)
            r.slope[:, cols] = (grad_act * r.slope[:, cols].astype(F32)).astype(LOW)

    move(gather_end, "up0")
    up_half(0)
    grad_wide(DOWN, r.cot, r.act, 0)
    move(reduce_b, "dn0")
    move(gather_end, "up1")
    up_half(half)
    grad_wide(DOWN, r.cot, r.act, half)
    move(reduce_b, "dn1")
    everything = pl.ds(0, g.ff)
    move(gather_end, "dn0")
    down_half(0)
    grad_wide(UP, r.a3, r.slope, 0)
    move(reduce_b, "up0")
    move(gather_turned, "dn1")
    down_half(half)
    exchange_start(2, lambda rows: dot(r.slope[rows], wide(UP, everything), 1, 1))
    grad_wide(UP, r.a3, r.slope, half)
    move(reduce_b, "up1")

    def after_up(rows, total):
        grad = r.cot[rows].astype(F32) + norm_back(2, r.resid_two[rows], total)
        r.grad[rows] = grad
        r.grad_low[rows] = grad.astype(LOW)

    move(reduce_a, "dn0")
    by_rows(2, after_up)
    put8(CO, dot(r.grad_low[...], r.cmixed[...], 0, 0))
    move(reduce_b, "co")
    r.g_mixed[...] = dot(r.grad_low[...], w8(CO), 1, 0).astype(LOW)

    def cross_back(m):
        @pl.loop(0, pairs)
        def _(h):
            lanes = pl.ds(pl.multiple_of(h * PAIR, PAIR), PAIR)
            queries, grads, soft = [], [], []
            for n in range(g.row_mb):
                row = m * g.row_mb + n
                rows = pl.ds(row * g.seq, g.seq)
                image = m * g.img_mb + r.image_ids[m, n]
                grads.append(stack_heads(r.g_mixed[rows, lanes], masks))
                queries.append(stack_heads(r.cq[rows, lanes], masks))
                weights_low = r.cross_p[row * pairs + h]
                soft.append(weights_low)
                prob = weights_low.astype(F32)
                grad_p = dot(r.kv[1, image, :, lanes], grads[-1], 1, 1)
                inner = jnp.sum(prob * grad_p, axis=0, keepdims=True)
                grad_s = (prob * (grad_p - inner)).astype(LOW)
                r.cross_ds[:, lanes_of(n)] = grad_s
                grad_q = join_heads(dot(grad_s, r.kv[0, image, :, lanes], 0, 0)) * score_scale
                r.cq[rows, lanes] = grad_q.astype(LOW)
            soft = jnp.concatenate(soft, axis=1)
            chosen = [
                [
                    jnp.where(r.image_ids[m, n] == i, jnp.ones((1, PAIR), F32), 0.0).astype(LOW)
                    for i in range(g.img_mb)
                ]
                for n in range(g.row_mb)
            ]

            def picked(parts):
                return jnp.concatenate(
                    [jnp.concatenate([v * c for c in cs], axis=1) for v, cs in zip(parts, chosen)], axis=0
                )

            for j, left, parts, scale in ((0, r.cross_ds[...], queries, score_scale), (1, soft, grads, 1.0)):
                both = dot(left, picked(parts), 1, 0)
                for i in range(g.img_mb):
                    part = both[:, i * PAIR:(i + 1) * PAIR] * scale
                    r.kv[j, m * g.img_mb + i, :, lanes] = part.astype(LOW)

    cross_back(0)
    move(reduce_on, "dn1", reduce_z, "dn0", reduce_a, "up0")
    cross_back(1)
    move(reduce_a, "up1", reduce_on, "co", reduce_z, "up0")
    exchange_start(3, lambda rows: dot(r.cq[rows], w8(CQ), 1, 1))
    def grad_images(j):
        put8(CKV + j, dot(r.enc[...], r.kv[j].reshape(g.images * g.ctx, g.f), 0, 0))

    put8(CQ, dot(r.a2[...], r.cq[...], 0, 0))
    move(reduce_b, "cq")
    move(reduce_turn, "dn1")
    grad_images(0)
    move(reduce_b, "ck")
    move(reduce_on, "dn0", reduce_z, "up1")
    grad_images(1)
    move(reduce_b, "cv")
    def after_query(rows, total):
        grad = r.grad[rows] + norm_back(1, r.resid_one[rows], total)
        r.grad[rows] = grad
        r.grad_low[rows] = grad.astype(LOW)

    move(reduce_turn, "co", reduce_a, "dn1", reduce_a, "cq")
    by_rows(3, after_query)
    move(reduce_on, "up0")
    put8(SO, dot(r.grad_low[...], r.mixed[...], 0, 0))
    move(reduce_b, "so")
    r.g_mixed[...] = dot(r.grad_low[...], w8(SO), 1, 0).astype(LOW)

    def self_back(first, last):
        @pl.loop(first, last)
        def _(p):
            rows = pl.ds(pl.multiple_of(p * PAIR, PAIR), PAIR)
            for h in range(pairs):
                lanes = lanes_of(h)
                queries = stack_heads(r.qkv[0, rows, lanes], masks)
                grads = stack_heads(r.g_mixed[rows, lanes], masks)
                weights_low = r.self_p[p, h]
                prob = weights_low.astype(F32)
                grad_p = dot(r.qkv[2, rows, lanes], grads, 1, 1)
                inner = jnp.sum(prob * grad_p, axis=0, keepdims=True)
                grad_s = (prob * (grad_p - inner)).astype(LOW)
                grad_q = join_heads(dot(grad_s, r.qkv[1, rows, lanes], 0, 0)) * score_scale
                grad_k = dot(grad_s, queries, 1, 0) * score_scale
                grad_v = dot(weights_low, grads, 1, 0)
                r.qkv[0, rows, lanes] = grad_q.astype(LOW)
                r.qkv[1, rows, lanes] = grad_k.astype(LOW)
                r.qkv[2, rows, lanes] = grad_v.astype(LOW)

    move(reduce_a, "ck")
    self_back(0, g.t // PAIR)
    move(reduce_on, "up1", reduce_z, "cq")
    exchange_start(
        4,
        lambda rows: dot(r.qkv[0, rows], w8(QKV), 1, 1)
        + dot(r.qkv[1, rows], w8(QKV + 1), 1, 1)
        + dot(r.qkv[2, rows], w8(QKV + 2), 1, 1),
    )
    for_name = ("q", "k", "v")

    def grad_project(j):
        put8(QKV + j, dot(r.a1[...], r.qkv[j], 0, 0))
        move(reduce_b, for_name[j])

    def after_qkv(rows, total):
        r.grad[rows] = r.grad[rows] + norm_back(0, r.hidden[rows].astype(F32), total)

    move(reduce_z, "ck", reduce_a, "cv", reduce_a, "co")
    grad_project(0)
    grad_project(1)
    grad_project(2)
    by_rows(4, after_qkv)
    write(r.grad, r.in_grad)
    move(reduce_on, "cq", reduce_on, "ck", reduce_a, "so", reduce_z, "cv")
    for i in range(3):
        r.gain_total[0, i:i + 1] = jnp.sum(r.gain_sum[i], axis=0, keepdims=True)
    if g.comm:
        first = len(small)
        for k in hops:
            meet(r.gain_total.at[0], r.total_land.at[k], at_z[k])

    def features(j, h):
        if g.comm:
            return r.w8[j, pl.ds(h * (g.nz // 2), g.nz // 2)].reshape(g.d // 2, g.f)
        return r.w8[j, pl.ds(pl.multiple_of(h * (g.d // 2), g.d // 2), g.d // 2)]

    def encoder_part(image, h):
        return dot(r.kv[0, image], features(CKV, h), 1, 1) + dot(r.kv[1, image], features(CKV + 1, h), 1, 1)

    strips = g.d // 2 // PAIR

    def encoder_keep(image, value):
        for h in range(strips):
            r.cross_p[image * strips + h] = value[:, h * PAIR:(h + 1) * PAIR].astype(LOW)

    def encoder_copy(image):
        part = pl.ds(image * strips, strips)
        return remote(r.cross_p.at[part], r.enc_land.at[part], r.enc_s.at[image], r.enc_r.at[image], sibling)

    def encoder_leave():
        @pl.loop(0, g.images)
        def _(image):
            encoder_keep(image, encoder_part(image, 1 - mp))

        for image in range(g.images):
            encoder_copy(image).start()

    def encoder_join():
        for image in range(g.images):
            encoder_copy(image).wait_recv()
            encoder_copy(image).wait_send()

        @pl.loop(0, g.images)
        def _(image):
            landed = jnp.concatenate([r.enc_land[image * strips + h] for h in range(strips)], axis=1)
            encoder_keep(image, encoder_part(image, mp) + landed.astype(F32))

        for image in range(g.images):
            for h in range(strips):
                rows = pl.ds(image * g.ctx, g.ctx)
                write(r.cross_p.at[image * strips + h], r.enc_grad.at[rows, lanes_of(h)])

    def after_down(rows, total):
        r.a3[rows] = (r.resid_two[rows] + total).astype(LOW)

    encoder_leave()
    move(reduce_a, "q")
    exchange_start(5, lambda rows: dot(r.act[rows], wide(DOWN, everything), 1, 1))
    move(reduce_on, "cv", reduce_z, "so")
    if g.comm:
        total = r.gain_total[0]
        for k in hops:
            small[first + k].wait_recv()
            total = total + r.total_land[k]
        r.gain_total[1] = total
        hop = meet(r.gain_total.at[1], r.total_land.at[3], at_x)
    move(
        reduce_end, "dn1", reduce_end, "dn0", reduce_end, "up0", reduce_end, "up1", reduce_end, "co",
        reduce_end, "cq", reduce_end, "ck",
    )
    encoder_join()
    move(reduce_on, "so", reduce_z, "q", reduce_a, "k", reduce_a, "v")
    by_rows(5, after_down)
    write(r.a3, r.out)
    move(reduce_end, "cv")
    if g.comm:
        hop.wait_recv()
        r.gain_total[2] = r.gain_total[1] + r.total_land[3]
        hop = meet(r.gain_total.at[2], r.total_land.at[4], at_y)
    move(reduce_end, "so", reduce_z, "k", reduce_z, "v", reduce_end, "q")
    if g.comm:
        hop.wait_recv()
        total = r.gain_total[2] + r.total_land[4]
    if g.comm:
        spot = lax.broadcasted_iota(jnp.int32, (g.d, g.blk), 1) + me * g.blk
        place = jnp.where(spot == lax.broadcasted_iota(jnp.int32, (g.d, g.blk), 0), 1.0, 0.0)
        mine = lax.dot_general(
            total, place, (((1,), (0,)), ((), ())), precision=lax.Precision.HIGHEST, preferred_element_type=F32
        )
        r.gain_out[...] = mine[0:3]
    else:
        r.gain_out[...] = r.gain_total[0, 0:3]
    move(reduce_end, "k", reduce_end, "v")
    for copy in written:
        copy.wait()
    for copy in small:
        copy.wait_send()
    for copy, condition in started:
        only(condition, copy.wait_send)


def run_layer(g, operands):
    vmem = pl.BlockSpec(memory_space=pltpu.VMEM)
    smem = pl.BlockSpec(memory_space=pltpu.SMEM)
    anywhere = pl.BlockSpec(memory_space=pl.ANY)
    shape = jax.ShapeDtypeStruct
    ins = dict(
        image_ids=smem, seg=vmem, hidden_in=anywhere, gains_in=vmem, cot_in=anywhere, enc_in=anywhere,
        qkv_in=anywhere, so_in=anywhere, cq_in=anywhere, ckv_in=anywhere, co_in=anywhere,
        up_in=anywhere, down_in=anywhere,
    )
    outs = dict(
        out=(shape((g.t, g.d), LOW), anywhere),
        in_grad=(shape((g.t, g.d), F32), anywhere),
        enc_grad=(shape((g.images * g.ctx, g.d // 2), LOW), anywhere),
        gain_out=(shape((3, g.blk if g.comm else g.d), F32), vmem),
    )
    grid = (g.nz, 4, g.blk) if g.comm else (g.d,)
    dma = pltpu.SemaphoreType.DMA
    scratch = dict(
        w8=pltpu.VMEM((MATS, *grid, g.f), LOW),
        wf=pltpu.VMEM((2, *grid, g.ff), LOW),
        hidden=pltpu.VMEM((g.t, g.d), LOW),
        enc=pltpu.VMEM((g.images * g.ctx, g.d), LOW),
        cot=pltpu.VMEM((g.t, g.d), LOW),
        gains=pltpu.VMEM((3, 1, g.d), F32),
        gain_sum=pltpu.VMEM((3, 8, g.d), F32),
        gain_total=pltpu.VMEM((3, 8, g.d), F32),
        bias=pltpu.VMEM((g.t // PAIR, PAIR, PAIR), F32),
        a1=pltpu.VMEM((g.t, g.d), LOW),
        a2=pltpu.VMEM((g.t, g.d), LOW),
        a3=pltpu.VMEM((g.t, g.d), LOW),
        qkv=pltpu.VMEM((3, g.t, g.f), LOW),
        mixed=pltpu.VMEM((g.t, g.f), LOW),
        cq=pltpu.VMEM((g.t, g.f), LOW),
        cmixed=pltpu.VMEM((g.t, g.f), LOW),
        g_mixed=pltpu.VMEM((g.t, g.f), LOW),
        kv=pltpu.VMEM((2, g.images, g.ctx, g.f), LOW),
        self_p=pltpu.VMEM((g.t // PAIR, g.f // PAIR, PAIR, 2 * PAIR), LOW),
        cross_p=pltpu.VMEM((g.rows * (g.f // PAIR), g.ctx, PAIR), LOW),
        cross_ds=pltpu.VMEM((g.ctx, g.row_mb * PAIR), LOW),
        resid_one=pltpu.VMEM((g.t, g.d), F32),
        resid_two=pltpu.VMEM((g.t, g.d), F32),
        grad=pltpu.VMEM((g.t, g.d), F32),
        grad_low=pltpu.VMEM((g.t, g.d), LOW),
        act=pltpu.VMEM((g.t, g.ff), LOW),
        slope=pltpu.VMEM((g.t, g.ff), LOW),
        stage=pltpu.VMEM((2, g.t, g.d), LOW),
        land=pltpu.VMEM((3, g.t, g.d), LOW),
        enc_land=pltpu.VMEM((g.images * (g.d // 2 // PAIR), g.ctx, PAIR), LOW),
        local_sem=dma((10,)),
        ex_s=dma((6, 2)), ex_r=dma((6, 2)),
        enc_s=dma((g.images,)), enc_r=dma((g.images,)),
        write_sem=dma((16 + g.images * (g.d // 2 // PAIR),)),
    )
    if g.comm:
        outs.update(
            g8_out=(shape((MATS, g.blk, g.f), F32), anywhere),
            gf_out=(shape((2, g.blk, g.ff), F32), anywhere),
        )
        hops = g.nz - 1
        scratch.update(
            g8=pltpu.VMEM((MATS, g.blk, g.f), F32),
            gf=pltpu.VMEM((2, g.blk, g.ff), F32),
            p8=pltpu.VMEM((MATS, *grid, g.f), LOW),
            pf=pltpu.VMEM((2, *grid, g.ff), LOW),
            lb8=pltpu.VMEM((2, MATS - 1, g.nz, g.blk, g.f), LOW),
            lbf=pltpu.VMEM((2, 3, g.nz, g.blk, g.ff // 2), LOW),
            la8=pltpu.VMEM((MATS - 1, g.nz, g.blk, g.f), LOW),
            laf=pltpu.VMEM((3, g.nz, g.blk, g.ff // 2), LOW),
            lz8=pltpu.VMEM((hops, MATS - 1, g.blk, g.f), LOW),
            lzf=pltpu.VMEM((hops, 3, g.blk, g.ff // 2), LOW),
            lx8=pltpu.VMEM((MATS - 1, g.blk, g.f), LOW),
            lxf=pltpu.VMEM((3, g.blk, g.ff // 2), LOW),
            turnf_z=pltpu.VMEM((hops, 4, g.blk, g.ff // 2), LOW),
            turnf_x=pltpu.VMEM((4, g.blk, g.ff // 2), LOW),
            turnf_b=pltpu.VMEM((2, g.blk, g.ff // 2), LOW),
            turnf_a=pltpu.VMEM((g.blk, g.ff // 2), LOW),
            turn8_z=pltpu.VMEM((hops, 1, 4, g.blk, g.f), LOW),
            turn8_x=pltpu.VMEM((1, 4, g.blk, g.f), LOW),
            turn8_b=pltpu.VMEM((2, 1, g.blk, g.f), LOW),
            turn8_a=pltpu.VMEM((1, g.blk, g.f), LOW),
            gain_land=pltpu.VMEM((hops + 2, 16, g.d), LOW),
            gain_pass=pltpu.VMEM((3, 16, g.d), LOW),
            total_land=pltpu.VMEM((hops + 2, 8, g.d), F32),
            agz_s=dma((12, 4)), agz_r=dma((12, 4)),
            aga_s=dma((12, g.nz)), aga_r=dma((12, g.nz)),
            agb_s=dma((12, g.nz + 1)), agb_r=dma((12, g.nz + 1)),
            rsz_s=dma((12, 4)), rsz_r=dma((12, 4)),
            rsa_s=dma((12,)), rsa_r=dma((12,)),
            rsb_s=dma((12, 2)), rsb_r=dma((12, 2)),
            small_s=dma((2 * hops + 4,)), small_r=dma((2 * hops + 4,)),
        )
    else:
        outs.update(
            p8=(shape((MATS, g.d, g.f), LOW), vmem),
            pf=(shape((2, g.d, g.ff), LOW), vmem),
        )
    g.names = (*ins, *outs, *scratch)
    return dict(zip(outs, pl.pallas_call(
        functools.partial(layer, g),
        out_shape=[o[0] for o in outs.values()],
        in_specs=list(ins.values()),
        out_specs=[o[1] for o in outs.values()],
        scratch_shapes=list(scratch.values()),
        compiler_params=pltpu.CompilerParams(
            collective_id=0, has_side_effects=True, vmem_limit_bytes=63 * 2**20
        ),
        name="layer",
    )(*operands)))


def pass_on(g, out, in_grad, enc, gain, g8, gf, *refs):
    outs, (v_out, v_in, v_gain, v_g8, v_gf, low, full, in_sem, out_sem) = refs[:11], refs[11:]
    coming, leaving = [], []

    def bring(src, dst):
        coming.append(pltpu.make_async_copy(src, dst, in_sem.at[len(coming)]))
        coming[-1].start()

    def leave(src, dst):
        leaving.append(pltpu.make_async_copy(src, dst, out_sem.at[len(leaving)]))
        leaving[-1].start()

    halves = [pl.ds(i * g.t // 2, g.t // 2) for i in range(2)]
    images = [pl.ds(i * g.ctx, g.ctx) for i in range(g.images)]
    for rows in images:
        bring(enc.at[rows], low.at[rows])
    for rows in halves:
        bring(in_grad.at[rows], v_in.at[rows])
    bring(out, v_out)
    bring(g8, v_g8)
    bring(gf, v_gf)
    bring(gain, v_gain)
    for i, rows in enumerate(images):
        coming[i].wait()
        full[rows] = low[rows].astype(F32)
        leave(full.at[rows], outs[2].at[rows])
    for copy, rows in zip(coming[g.images:], halves):
        copy.wait()
        leave(v_in.at[rows], outs[1].at[rows])
    for copy in coming[g.images + 2:]:
        copy.wait()
    leave(v_out, outs[0])
    leave(v_gain, outs[3])
    for src, dst in zip(
        (v_g8.at[pl.ds(QKV, 3)], v_g8.at[SO], v_g8.at[CQ], v_g8.at[pl.ds(CKV, 2)], v_g8.at[CO], v_gf.at[UP], v_gf.at[DOWN]),
        outs[4:],
    ):
        leave(src, dst)
    for copy in leaving:
        copy.wait()


def hand_over(g, o):
    shape = jax.ShapeDtypeStruct
    tokens, enc = (g.t, g.d), (g.images * g.ctx, g.d // 2)
    one, wide = (g.blk, g.f), (g.blk, g.ff)
    shapes = (tokens, tokens, enc, (3, g.blk), (3, *one), one, one, (2, *one), one, wide, wide)
    anywhere = pl.BlockSpec(memory_space=pl.ANY)
    dma = pltpu.SemaphoreType.DMA
    return pl.pallas_call(
        functools.partial(pass_on, g),
        out_shape=[shape(s, LOW if i == 0 else F32) for i, s in enumerate(shapes)],
        in_specs=[anywhere] * 6,
        out_specs=[anywhere] * 11,
        scratch_shapes=[
            pltpu.VMEM(tokens, LOW), pltpu.VMEM(tokens, F32), pltpu.VMEM((3, g.blk), F32),
            pltpu.VMEM((MATS, *one), F32), pltpu.VMEM((2, *wide), F32),
            pltpu.VMEM(enc, LOW), pltpu.VMEM(enc, F32), dma((g.images + 6,)), dma((g.images + 11,)),
        ],
        compiler_params=pltpu.CompilerParams(vmem_limit_bytes=63 * 2**20),
        name="hand_over",
    )(o["out"], o["in_grad"], o["enc_grad"], o["gain_out"], o["g8_out"], o["gf_out"])


def body(
    dp, mp, hidden, encoder_tokens, segment_ids, image_index, cotangent, norm_gains, qkv_weight,
    self_out_weight, cross_query_weight, cross_kv_weight, cross_out_weight, up_weight, down_weight,
):
    micro, row_mb, seq, d = hidden.shape
    img_mb, ctx = encoder_tokens.shape[1:3]
    blk, f = self_out_weight.shape
    g = SimpleNamespace(
        micro=micro, row_mb=row_mb, seq=seq, d=d, img_mb=img_mb, ctx=ctx, blk=blk, f=f,
        ff=up_weight.shape[1], rows=micro * row_mb, t=micro * row_mb * seq, images=micro * img_mb,
        nz=dp // 4, comm=dp == 16 and blk % 16 == 0,
    )
    weights = [
        qkv_weight, self_out_weight, cross_query_weight, cross_kv_weight, cross_out_weight, up_weight, down_weight,
    ]
    gains = norm_gains
    if not g.comm:
        gains = lax.all_gather(norm_gains, "dp", axis=1, tiled=True)
        weights = [lax.all_gather(w, "dp", axis=w.ndim - 2, tiled=True) for w in weights]
    for i in (1, 2, 4):
        weights[i] = weights[i][None]
    o = run_layer(g, (
        image_index, segment_ids, hidden.reshape(g.t, d), gains, cotangent.reshape(g.t, d),
        encoder_tokens.reshape(g.images * ctx, d), *weights,
    ))
    if g.comm:
        whole = hand_over(g, o)
    else:
        small = lax.psum_scatter(o["p8"].astype(F32), "dp", scatter_dimension=1, tiled=True)
        wide = lax.psum_scatter(o["pf"].astype(F32), "dp", scatter_dimension=1, tiled=True)
        whole = (
            o["out"], o["in_grad"], o["enc_grad"].astype(F32),
            lax.psum_scatter(o["gain_out"], "dp", scatter_dimension=1, tiled=True),
            small[QKV:QKV + 3], small[SO], small[CQ], small[CKV:CKV + 2], small[CO], wide[UP], wide[DOWN],
        )
    return (
        whole[0].reshape(hidden.shape), whole[1].reshape(hidden.shape),
        whole[2].reshape(micro, img_mb, ctx, d // 2), *whole[3:],
    )


def solution(mesh):
    tokens, kept = P(None, "dp", None, None), P("dp", "mp")
    three = P(None, "dp", "mp")
    return jax.shard_map(
        functools.partial(body, mesh.shape["dp"], mesh.shape["mp"]),
        mesh=mesh,
        in_specs=(
            tokens, tokens, P(None, "dp", None), P(None, "dp"), tokens, P(None, "dp"),
            three, kept, kept, three, kept, kept, kept,
        ),
        out_specs=(
            tokens, tokens, P(None, "dp", None, "mp"), P(None, "dp"),
            three, kept, kept, three, kept, kept, kept,
        ),
        check_vma=False,
    )
```

profile of v0, /device:TPU:0, one launch (start us, length us, event | category | flops | bytes accessed | tf_op | source)
XLA Modules:
  0.0 171.0 jit_solution(12071868493062656829)
XLA Ops:
  0.6 164.9 %layer.1 = (bf16[512,768]{1,0:T(8,128)(2,1)}, f32[512,768]{1,0:T(8,128)}, bf16[2304,384]{1,0:T(8,128)(2,1)}, f32[3,48]{1,0:T(4,128)}, f32[8,48,384]{2,1,0:T(8,128)}, /*index=5*/f32[2,48,1536]{2,1,0:T(8,128)}) custom-call(s32[2,4]{1,0:T(2,128)} %refs_0_.1, s32[2,4,64]{2,1,0:T(4,128)} %refs_1_.1, bf16[512,768]{1,0:T(8,128)(2,1)} %bitcast.10, ...), custom_call_target="tpu_custom_call" | custom-call | tf_op jit(solution)/shard_map/layer/pallas_call | solution.py:943
  165.5 5.2 %hand_over.1 = (bf16[512,768]{1,0:T(8,128)(2,1)}, f32[512,768]{1,0:T(8,128)}, f32[2304,384]{1,0:T(8,128)}, f32[3,48]{1,0:T(4,128)}, f32[3,48,384]{2,1,0:T(8,128)...) custom-call(bf16[512,768]{1,0:T(8,128)(2,1)} %get-tuple-element.28.o, ...), custom_call_target="tpu_custom_call" | custom-call | tf_op jit(solution)/shard_map/hand_over/pallas_call | solution.py:1005
where the time goes:
time: 171 us
  Pallas kernels  170 us (99%)
    pallas_call x1, Pallas kernels, run_layer(): pl.pallas_call(functools.partial(layer, g), out_shape=[o[0] for o in outs...  165 us
    pallas_call x1, Pallas kernels, hand_over(): pl.pallas_call(functools.partial(pass_on, g), out_shape=[shape(s, LOW if...  5.24 us

commit v1 on v0

--- a/solution.py
+++ b/solution.py
@@ -283,7 +283,7 @@
         if t.turned:
             z_start(t, t.p_row, t.tz)
             return
-        for k, c in enumerate((col_b, col_d)):
+        for k, c in ((1, col_d), (0, col_b)):
             start(remote(t.p_column(c), t.lb(k), r.rsb_s.at[t.i, k], r.rsb_r.at[t.i, k], at_b))
 
     def reduce_on(name):
@@ -329,7 +329,7 @@
                 target = t.p(zi, c)
                 target[...] = added(target, t.in_row(t.tz(2), c)).astype(LOW)
 
-        for k, c in enumerate((col_b, col_d)):
+        for k, c in ((1, col_d), (0, col_b)):
             start(remote(t.p(zi, c), t.tb(k), r.rsb_s.at[t.i, k], r.rsb_r.at[t.i, k], at_b))
 
     def reduce_a(name):

time: 171 us -> 171 us (level)
  no operation moved by 1% of the time
where the time goes in v1:
time: 171 us
  Pallas kernels  170 us (99%)
    pallas_call x1, Pallas kernels, run_layer(): pl.pallas_call(functools.partial(layer, g), out_shape=[o[0] for o in outs...  165 us
    pallas_call x1, Pallas kernels, hand_over(): pl.pallas_call(functools.partial(pass_on, g), out_shape=[shape(s, LOW if...  5.24 us

profile of v1, /device:TPU:0, one launch (start us, length us, event | category | flops | bytes accessed | tf_op | source)
XLA Modules:
  0.0 171.2 jit_solution(3653307916911214944)
XLA Ops:
  0.6 165.2 %layer.1 = (bf16[512,768]{1,0:T(8,128)(2,1)}, f32[512,768]{1,0:T(8,128)}, bf16[2304,384]{1,0:T(8,128)(2,1)}, f32[3,48]{1,0:T(4,128)}, f32[8,48,384]{2,1,0:T(8,128)}, /*index=5*/f32[2,48,1536]{2,1,0:T(8,128)}) custom-call(s32[2,4]{1,0:T(2,128)} %refs_0_.1, s32[2,4,64]{2,1,0:T(4,128)} %refs_1_.1, bf16[512,768]{1,0:T(8,128)(2,1)} %bitcast.10, ...), custom_call_target="tpu_custom_call" | custom-call | tf_op jit(solution)/shard_map/layer/pallas_call | solution.py:943
  165.8 5.2 %hand_over.1 = (bf16[512,768]{1,0:T(8,128)(2,1)}, f32[512,768]{1,0:T(8,128)}, f32[2304,384]{1,0:T(8,128)}, f32[3,48]{1,0:T(4,128)}, f32[3,48,384]{2,1,0:T(8,128)...) custom-call(bf16[512,768]{1,0:T(8,128)(2,1)} %get-tuple-element.28.o, ...), custom_call_target="tpu_custom_call" | custom-call | tf_op jit(solution)/shard_map/hand_over/pallas_call | solution.py:1005
